TPU v7x, 128 devices: a whole 4x4x4 slice. The times are simulated.
128 devices in a mesh: row: 16 (over z, x), col: 8 (over y, core).
Axes of the slice: x: 4, y: 4, z: 4, core: 2. Of those that a mesh axis runs over, the one named last changes fastest.
Arguments:
- leaf_mass: bfloat16 [128, 2048, 2048], P(('row', 'col')), as said below
- tile_mask: int32 [128, 16, 16], P(('row', 'col')), may hold values from 0 to 1, as said below
- constraint_modes: bfloat16 [128, 2048, 1024], P(('row', 'col')), may hold values from -0.125 to 0.125
- leaf_fixed_modes: bfloat16 [128, 2048, 128], P(('row', 'col')), may hold values from -6 to 6
- block_map: int32 [128, 2, 4], P(('row', 'col')), may hold values from 0 to 3, each once within a row
- group_mass: float32 [8, 512, 512], P('col', 'row'), as said below
- top_mass: float32 [512, 512], P(('row', 'col')), as said below
- group_basis: float32 [8, 512, 128], P('col', 'row'), may hold values from -6 to 6
- top_basis: float32 [512, 128], P('row'), may hold values from -6 to 6
Outputs:
- coupling: float32 [128, 128, 2, 128], P(('row', 'col'))
- group_modes: float32 [8, 512, 128], P('col', 'row')
- top_modes: float32 [512, 128], P('row')
- group_assembled: float32 [8, 512, 512], P('col', 'row')
- apex_gathered_mass: float32 [512, 512], P(('row', 'col'))
Inputs may be any that keep to these rules, and one draw needn't show every extreme that they name: `tile_mask`: symmetric in its two tile indices, with ones on the diagonal tiles. block_map[l, k] is a permutation of the 4 separator blocks. `leaf_mass`: each leaf's matrix is symmetric and strictly diagonally dominant with a positive diagonal. `group_mass`: each group's matrix is symmetric and strictly diagonally dominant with a positive diagonal. `top_mass`: symmetric and strictly diagonally dominant with a positive diagonal.
All inputs are finite; a program needn't handle non-finite values.
Results may differ from a plain program's by a relative error of at most 0.0029.
Values sent between devices are 32-bit elements; how exact they have to be, the bound alone decides.
A program may use at most 128 MiB of HBM per device.

v0:
```python
import jax
import jax.numpy as jnp
from jax import lax
from jax.sharding import PartitionSpec as P

TILE = 128
SEP = 512
SEP_BLOCK = 128


def copy_for_each(value, axis):
    peers = lax.axis_size(axis)
    return lax.all_to_all(
        jnp.broadcast_to(value[None], (peers, *value.shape)), axis, 0, 0, tiled=True
    )


def joined_along(parts, dim):
    lengths = list(parts.shape[1:])
    lengths[dim] *= parts.shape[0]
    return jnp.moveaxis(parts, 0, dim).reshape(lengths)


def gather_directly(value, axis, dim):
    parts = copy_for_each(value, axis)
    return joined_along(parts, dim)


def sent_together(arrays, axis, dim, along):
    widths = [a.shape[along] for a in arrays]
    both = jnp.concatenate(arrays, axis=along)
    filled = gather_directly(both, axis, dim)
    return tuple(jnp.split(filled, [sum(widths[:k]) for k in range(1, len(widths))], axis=along))


def in_blocks(value, dim, peers):
    before, after = (value.shape[:dim], value.shape[dim + 1 :])
    return jnp.moveaxis(value.reshape(*before, peers, -1, *after), dim, 0)


def sent_and_summed(value, axis, dim):
    peers = lax.axis_size(axis)
    parts = lax.all_to_all(in_blocks(value, dim, peers), axis, 0, 0, tiled=True)
    return jnp.sum(parts, axis=0)


def sent_together_2(arrays, axis, dim, along):
    widths = [a.shape[along] for a in arrays]
    both = jnp.concatenate(arrays, axis=along)
    filled = sent_and_summed(both, axis, dim)
    return tuple(jnp.split(filled, [sum(widths[:k]) for k in range(1, len(widths))], axis=along))


def taken_together(value, axis):
    return copy_for_each(value, axis).sum(axis=0)


def in_one(arrays, axis):
    ends = [0]
    for a in arrays:
        ends.append(ends[-1] + a.size)
    total = taken_together(jnp.concatenate([a.ravel() for a in arrays]), axis)
    return tuple((total[b:e].reshape(a.shape) for a, b, e in zip(arrays, ends, ends[1:])))


def contract_product(left_side, right_side):
    return lax.dot_general(
        left_side, right_side, (((0,), (0,)), ((), ())), preferred_element_type=jnp.float32
    )


def to_separator(partial_value, ordering):
    block_count = SEP // SEP_BLOCK
    inverse = jnp.argsort(ordering)
    blocks = partial_value.reshape(block_count, SEP_BLOCK, block_count, SEP_BLOCK)
    blocks = blocks[inverse][:, :, inverse]
    return blocks.reshape(SEP, SEP)


def to_leaf(mode_rows, ordering):
    block_count = SEP // SEP_BLOCK
    blocks = mode_rows.reshape(block_count, SEP_BLOCK, mode_rows.shape[1])
    return blocks[ordering].reshape(SEP, mode_rows.shape[1])


def gram_terms(matrix_rows, basis_rows, basis_whole):
    applied = jnp.dot(matrix_rows, basis_whole, precision=lax.Precision.HIGHEST)
    return jnp.dot(basis_rows.T, applied, precision=lax.Precision.HIGHEST)


def from_gram(gram_matrix, basis_whole):
    gram_matrix = 0.5 * (gram_matrix + gram_matrix.T)
    lower_factor = jnp.linalg.cholesky(gram_matrix)
    return lax.linalg.triangular_solve(
        lower_factor, basis_whole, left_side=False, lower=True, transpose_a=True
    )


def body(
    leaf_mass,
    tile_mask,
    constraint_modes,
    leaf_fixed_modes,
    block_map,
    group_mass,
    top_mass,
    group_basis,
    top_basis,
):
    leaf_matrix = leaf_mass[0]
    leaf_rows = leaf_matrix.shape[0]
    tile_count = tile_mask.shape[1]
    chosen = tile_mask[0].astype(jnp.bfloat16)
    masked = (
        leaf_matrix.reshape(tile_count, TILE, tile_count, TILE) * chosen[:, None, :, None]
    ).reshape(leaf_rows, leaf_rows)
    modes_c = constraint_modes[0]
    loaded = jnp.dot(masked, modes_c, preferred_element_type=jnp.float32).astype(jnp.bfloat16)
    partial_group = to_separator(
        contract_product(modes_c[:, :SEP], loaded[:, :SEP]), block_map[0, 0]
    )
    partial_top = to_separator(contract_product(modes_c[:, SEP:], loaded[:, SEP:]), block_map[0, 1])
    projected = contract_product(leaf_fixed_modes[0], loaded)
    line_fraction = group_mass.shape[1]
    top_share = top_mass.shape[0]
    whole_group, whole_top = sent_together((group_basis[0], top_basis), "row", 0, 1)
    row_index = lax.axis_index("row")
    col_index = lax.axis_index("col")
    share_group, share_top = sent_together_2((partial_group, partial_top), "row", 0, 1)
    share_group = share_group + group_mass[0]
    top_rows = lax.dynamic_update_slice(
        jnp.zeros((line_fraction, SEP), jnp.float32),
        top_mass,
        (col_index * top_share, jnp.int32(0)),
    )
    share_top = taken_together(share_top + top_rows, "col")
    gram_group, gram_top = in_one(
        (
            gram_terms(share_group, group_basis[0], whole_group),
            gram_terms(share_top, top_basis, whole_top),
        ),
        "row",
    )
    top_kept = lax.dynamic_slice_in_dim(share_top, col_index * top_share, top_share, 0)
    modes_group = from_gram(gram_group, whole_group)
    modes_top = from_gram(gram_top, whole_top)
    first = jnp.dot(
        projected[:, :SEP], to_leaf(modes_group, block_map[0, 0]), precision=lax.Precision.HIGHEST
    )
    second = jnp.dot(
        projected[:, SEP:], to_leaf(modes_top, block_map[0, 1]), precision=lax.Precision.HIGHEST
    )
    coupling = jnp.stack([first, second], axis=1)[None]
    group_out = lax.dynamic_slice_in_dim(modes_group, row_index * line_fraction, line_fraction, 0)[
        None
    ]
    top_out = lax.dynamic_slice_in_dim(
        modes_top, row_index * top_basis.shape[0], top_basis.shape[0], 0
    )
    group_assembled = (SEP * share_group)[None]
    apex_gathered_mass = SEP * top_kept
    return (coupling, group_out, top_out, group_assembled, apex_gathered_mass)


def solution(mesh):
    in_specs = (
        P(("row", "col"), None, None),
        P(("row", "col"), None, None),
        P(("row", "col"), None, None),
        P(("row", "col"), None, None),
        P(("row", "col"), None, None),
        P("col", "row", None),
        P(("row", "col"), None),
        P("col", "row", None),
        P("row", None),
    )
    out_specs = (
        P(("row", "col"), None, None, None),
        P("col", "row", None),
        P("row", None),
        P("col", "row", None),
        P(("row", "col"), None),
    )
    return jax.shard_map(body, mesh=mesh, in_specs=in_specs, out_specs=out_specs, check_vma=False)
```

profile of v0, /device:TPU:1, one launch (start us, length us, event | category | flops | bytes accessed | tf_op | source)
XLA Modules:
  0.0 214.4 jit_solution(4026263986912305048)
XLA Ops:
  1.4 4.4 %mul.40 = bf16[16,128,16,128]{3,2,1,0:T(8,128)(2,1)} broadcast(bf16[16,16]{1,0:T(8,128)(2,1)S(1)} %convert_bitcast_fusion), dimensions={0,2} | broadcast | bytes 8389120 | tf_op jit(solution)/shard_map/mul | solution.py:115
  5.8 13.3 %mul.41 = bf16[1,2048,2048]{2,1,0:T(8,128)(2,1)} reshape(bf16[16,128,16,128]{3,2,1,0:T(8,128)(2,1)} %mul.40) | data formatting | bytes 16777216 | tf_op jit(solution)/shard_map/mul | solution.py:115
  19.1 15.9 %fusion.3 = bf16[2048,1024]{1,0:T(8,128)(2,1)S(1)} fusion(bf16[1,2048,2048]{2,1,0:T(8,128)(2,1)} %param.12, bf16[1,2048,2048]{2,1,0:T(8,128)(2,1)} %mul.41, bf16[1,2048,1024]{2,1,0:T(8,128)(2,1)} %param.14), kind=kOutput, calls=%fused_computation.9 | convolution fusion | flops 8596226048 | bytes 25165824 | tf_op jit(solution)/shard_map/dot_general | solution.py:118
  35.0 1.3 fusion.12
  36.3 2.3 %fusion.17 = f32[512,512]{0,1:T(8,128)} fusion(bf16[2048,1024]{1,0:T(8,128)(2,1)S(1)} %bitcast.125, bf16[2048,1024]{1,0:T(8,128)(2,1)S(1)} %fusion.3), kind=kOutput, calls=%fused_computation.18 | convolution fusion | flops 1073741824 | bytes 5242880 | tf_op jit(solution)/shard_map/dot_general | solution.py:67
  42.8 1.4 concatenate.14
  44.2 1.6 reshape.154
  48.5 2.7 %pad_maximum_fusion = f32[16,32,1024]{2,1,0:T(8,128)} fusion(f32[16,32,512]{2,1,0:T(8,128)S(1)} %concatenate.15, f32[16,32,512]{2,1,0:T(8,128)} %concatenate.14), kind=kLoop, calls=%fused_computation.16 | loop fusion | flops 524288 | bytes 4194304 | tf_op jit(solution)/shard_map/concatenate | solution.py:49
  51.3 8.6 %all-to-all-start = ((f32[16,32,1024]{2,1,0:T(8,128)}), f32[16,32,1024]{2,1,0:T(8,128)S(1)}, u32[]{:S(2)}, u32[]{:S(2)}) async-start(f32[16,32,1024]{2,1,0:T(8,128)} %pad_maximum_fusion), calls=%async_computation | async-start | bytes 4194304 | tf_op jit(solution)/shard_map/all_to_all | solution.py:43
  59.9 30.9 %all-to-all-done = f32[16,32,1024]{2,1,0:T(8,128)S(1)} async-done(((f32[16,32,1024]{2,1,0:T(8,128)}), f32[16,32,1024]{2,1,0:T(8,128)S(1)}, u32[]{:S(2)}, u32[]{:S(2)}) %all-to-all-start) | async-done | bytes 2097184 | tf_op jit(solution)/shard_map/all_to_all | solution.py:43
  91.6 3.8 %all-to-all-start.1 = ((f32[16,32,256]{2,1,0:T(8,128)}), f32[16,32,256]{2,1,0:T(8,128)S(1)}, u32[]{:S(2)}, u32[]{:S(2)}) async-start(f32[16,32,256]{2,1,0:T(8,128)} %broadcast_in_dim.18), calls=%async_computation.1 | async-start | bytes 1048576 | tf_op jit(solution)/shard_map/all_to_all | solution.py:13
  96.3 9.4 %all-to-all-done.1 = f32[16,32,256]{2,1,0:T(8,128)S(1)} async-done(((f32[16,32,256]{2,1,0:T(8,128)}), f32[16,32,256]{2,1,0:T(8,128)S(1)}, u32[]{:S(2)}, u32[]{:S(2)}) %all-to-all-start.1) | async-done | bytes 524320 | tf_op jit(solution)/shard_map/all_to_all | solution.py:13
  105.6 0.9 broadcast_in_dim.20
  106.5 6.8 %all-to-all-start.2 = ((f32[8,32,512]{2,1,0:T(8,128)}), f32[8,32,512]{2,1,0:T(8,128)S(1)}, u32[]{:S(2)}, u32[]{:S(2)}) async-start(f32[8,32,512]{2,1,0:T(8,128)} %broadcast_in_dim.20), calls=%async_computation.2 | async-start | bytes 1048576 | tf_op jit(solution)/shard_map/all_to_all | solution.py:13
  113.9 8.7 %all-to-all-done.2 = f32[8,32,512]{2,1,0:T(8,128)S(1)} async-done(((f32[8,32,512]{2,1,0:T(8,128)}), f32[8,32,512]{2,1,0:T(8,128)S(1)}, u32[]{:S(2)}, u32[]{:S(2)}) %all-to-all-start.2) | async-done | bytes 524320 | tf_op jit(solution)/shard_map/all_to_all | solution.py:13
  123.3 2.9 %broadcast_in_dim.21 = f32[16,1,32768]{2,1,0:T(1,128)} broadcast(f32[32768]{0:T(1024)S(1)} %pad_maximum_fusion.1), dimensions={2} | broadcast | bytes 2228224 | tf_op jit(solution)/shard_map/broadcast_in_dim | solution.py:14
  126.3 3.7 %all-to-all-start.3 = ((f32[16,1,32768]{2,1,0:T(1,128)}), f32[16,1,32768]{2,1,0:T(1,128)S(1)}, u32[]{:S(2)}, u32[]{:S(2)}) async-start(f32[16,1,32768]{2,1,0:T(1,128)} %broadcast_in_dim.21), calls=%async_computation.3 | async-start | bytes 4194304 | tf_op jit(solution)/shard_map/all_to_all | solution.py:13
  130.0 4.3 %convolution_bitcast_fusion = f32[128,1024]{0,1:T(8,128)} fusion(bf16[2048,1024]{1,0:T(8,128)(2,1)} %copy-done.1, bf16[1,2048,128]{2,1,0:T(8,128)(2,1)S(1)} %copy-done), kind=kOutput, calls=%fused_computation.19 | convolution fusion | flops 536870912 | bytes 5242880 | tf_op jit(solution)/shard_map/dot_general | solution.py:67
  134.9 26.0 %all-to-all-done.3 = f32[16,1,32768]{2,1,0:T(1,128)S(1)} async-done(((f32[16,1,32768]{2,1,0:T(1,128)}), f32[16,1,32768]{2,1,0:T(1,128)S(1)}, u32[]{:S(2)}, u32[]{:S(2)}) %all-to-all-start.3) | async-done | bytes 2097184 | tf_op jit(solution)/shard_map/all_to_all | solution.py:13
  160.9 1.4 reduce_sum.29
  162.6 11.7 %cholesky.44 = f32[128,128]{1,0:T(8,128)S(1)} custom-call(f32[128,128]{1,0:T(8,128)S(1)} %fusion.38), custom_call_target="Cholesky" | custom-call | tf_op jit(solution)/shard_map/jit(cholesky)/cholesky | solution.py:93
  175.7 9.8 %custom-call.6 = f32[1,128,128]{1,2,0:T(8,128)S(1)} custom-call(f32[1,128,128]{2,1,0:T(8,128)S(1)} %fusion.31), custom_call_target="InvertDiagBlocksLowerTriangular" | custom-call | tf_op jit(solution)/shard_map/triangular_solve/custom-call.0 | solution.py:94
  186.2 11.9 %cholesky.55 = f32[128,128]{1,0:T(8,128)S(1)} custom-call(f32[128,128]{1,0:T(8,128)S(1)} %fusion.36), custom_call_target="Cholesky" | custom-call | tf_op jit(solution)/shard_map/jit(cholesky)/cholesky | solution.py:93
  199.4 9.8 %custom-call.7 = f32[1,128,128]{1,2,0:T(8,128)S(1)} custom-call(f32[1,128,128]{2,1,0:T(8,128)S(1)} %fusion.32), custom_call_target="InvertDiagBlocksLowerTriangular" | custom-call | tf_op jit(solution)/shard_map/triangular_solve/custom-call.0 | solution.py:94
  (81 shorter events, 20.0 us)
Async XLA Ops:
  0.6 129.4 %copy-start = (bf16[1,2048,128]{2,1,0:T(8,128)(2,1)S(1)}, bf16[1,2048,128]{2,1,0:T(8,128)(2,1)}, u32[]{:S(2)}) copy-start(bf16[1,2048,128]{2,1,0:T(8,128)(2,1)} %param.15) | copy-start | bytes 1572868
  19.1 15.9 %copy-start.8 = (bf16[1,2048,1024]{2,1,0:T(8,128)(2,1)S(1)}, bf16[1,2048,1024]{2,1,0:T(8,128)(2,1)}, u32[]{:S(2)}) copy-start(bf16[1,2048,1024]{2,1,0:T(8,128)(2,1)} %param.14) | copy-start | bytes 12582916
  35.0 3.6 %copy-start.1 = (bf16[2048,1024]{1,0:T(8,128)(2,1)}, bf16[2048,1024]{1,0:T(8,128)(2,1)S(1)}, u32[]{:S(2)}) copy-start(bf16[2048,1024]{1,0:T(8,128)(2,1)S(1)} %fusion.3) | copy-start | bytes 12582916
  36.3 2.3 %copy-start.7 = (s32[1,2,4]{2,1,0:T(2,128)S(1)}, s32[1,2,4]{2,1,0:T(2,128)}, u32[]{:S(2)}) copy-start(s32[1,2,4]{2,1,0:T(2,128)} %param.16) | copy-start | bytes 100
  48.5 11.3 %copy-start.4 = (f32[1,32,128]{2,1,0:T(8,128)S(1)}, f32[1,32,128]{2,1,0:T(8,128)}, u32[]{:S(2)}) copy-start(f32[1,32,128]{2,1,0:T(8,128)} %param.19) | copy-start | bytes 49156
  48.5 11.3 %copy-start.5 = (f32[32,128]{1,0:T(8,128)S(1)}, f32[32,128]{1,0:T(8,128)}, u32[]{:S(2)}) copy-start(f32[32,128]{1,0:T(8,128)} %param.20) | copy-start | bytes 49156
  51.3 44.3 %copy-start.3 = (f32[1,32,512]{2,1,0:T(8,128)S(1)}, f32[1,32,512]{2,1,0:T(8,128)}, u32[]{:S(2)}) copy-start(f32[1,32,512]{2,1,0:T(8,128)} %param.17) | copy-start | bytes 196612
  51.3 45.0 %copy-start.6 = (f32[4,512]{1,0:T(4,128)S(1)}, f32[4,512]{1,0:T(4,128)}, u32[]{:S(2)}) copy-start(f32[4,512]{1,0:T(4,128)} %param.18) | copy-start | bytes 24580
  51.3 39.5 %all-to-all-start = ((f32[16,32,1024]{2,1,0:T(8,128)}), f32[16,32,1024]{2,1,0:T(8,128)S(1)}, u32[]{:S(2)}, u32[]{:S(2)}) async-start(f32[16,32,1024]{2,1,0:T(8,128)} %pad_maximum_fusion), calls=%async_computation | async-start | bytes 4194304 | tf_op jit(solution)/shard_map/all_to_all | solution.py:43
  91.6 14.0 %all-to-all-start.1 = ((f32[16,32,256]{2,1,0:T(8,128)}), f32[16,32,256]{2,1,0:T(8,128)S(1)}, u32[]{:S(2)}, u32[]{:S(2)}) async-start(f32[16,32,256]{2,1,0:T(8,128)} %broadcast_in_dim.18), calls=%async_computation.1 | async-start | bytes 1048576 | tf_op jit(solution)/shard_map/all_to_all | solution.py:13
  106.5 16.1 %all-to-all-start.2 = ((f32[8,32,512]{2,1,0:T(8,128)}), f32[8,32,512]{2,1,0:T(8,128)S(1)}, u32[]{:S(2)}, u32[]{:S(2)}) async-start(f32[8,32,512]{2,1,0:T(8,128)} %broadcast_in_dim.20), calls=%async_computation.2 | async-start | bytes 1048576 | tf_op jit(solution)/shard_map/all_to_all | solution.py:13
  126.3 34.6 %all-to-all-start.3 = ((f32[16,1,32768]{2,1,0:T(1,128)}), f32[16,1,32768]{2,1,0:T(1,128)S(1)}, u32[]{:S(2)}, u32[]{:S(2)}) async-start(f32[16,1,32768]{2,1,0:T(1,128)} %broadcast_in_dim.21), calls=%async_computation.3 | async-start | bytes 4194304 | tf_op jit(solution)/shard_map/all_to_all | solution.py:13
  162.3 48.3 %copy-start.2 = (f32[128,1024]{0,1:T(8,128)S(1)}, f32[128,1024]{0,1:T(8,128)}, u32[]{:S(2)}) copy-start(f32[128,1024]{0,1:T(8,128)} %convolution_bitcast_fusion) | copy-start | bytes 1572868
where the time goes:
time: 216 us; the launch traced here: 214 us
  waiting for transfers between devices  75 us (35%)
  other arithmetic  53.8 us (25%)
  local copies, waits for them, and re-layouts  34.9 us (16%)
  matrix products  26.8 us (12%)
  starting transfers between devices  22.9 us (11%)
    all_to_all x3, waiting for transfers between devices, copy_for_each(): lax.all_to_all(jnp.broadcast_to(value[None], (peers, *value.shape)), axis...  44 us
    all_to_all x1, waiting for transfers between devices, sent_and_summed(): parts = lax.all_to_all(in_blocks(value, dim, peers), axis, 0, 0, tiled=True)  30.9 us
    another operation x6, other arithmetic, from_gram(): lower_factor = jnp.linalg.cholesky(gram_matrix)  25 us
    another operation x4, other arithmetic, from_gram(): lax.linalg.triangular_solve(lower_factor, basis_whole, left_side=False, l...  20.9 us
    mul x2, local copies, waits for them, and re-layouts, body(): leaf_matrix.reshape(tile_count, TILE, tile_count, TILE)  17.7 us
    dot_general x1, matrix products, body(): jnp.dot(masked, modes_c, preferred_element_type=jnp.float32)  15.9 us
    all_to_all x3, starting transfers between devices, copy_for_each(): lax.all_to_all(jnp.broadcast_to(value[None], (peers, *value.shape)), axis...  14.3 us
    all_to_all x1, starting transfers between devices, sent_and_summed(): parts = lax.all_to_all(in_blocks(value, dim, peers), axis, 0, 0, tiled=True)  8.55 us
  transfers between devices with their start and end apart: 4, of which 4 were waited for; matrix products, arithmetic and copies ran while one was open for 3% of the time, Pallas kernels for 0%

commit v1 on v0

v1 whole, which is shorter than its diff:
```python
import jax
import jax.numpy as jnp
from jax import lax
from jax.experimental import pallas as pl
from jax.experimental.pallas import tpu as pltpu
from jax.sharding import PartitionSpec as P

TILE = 128
SEP = 512
ROWS = 16
COLS = 8
N = 2048
CHUNK = 256
CHUNKS = N // CHUNK
F32 = jnp.float32
BF16 = jnp.bfloat16
MESH = pl.DeviceIdType.MESH
HIGHEST = lax.Precision.HIGHEST


def dot_tn(a, b, **kw):
    return lax.dot_general(a, b, (((0,), (0,)), ((), ())), preferred_element_type=F32, **kw)


def dot_nt(a, b, **kw):
    return lax.dot_general(a, b, (((1,), (1,)), ((), ())), preferred_element_type=F32, **kw)


def dot_nn(a, b, **kw):
    return jnp.dot(a, b, preferred_element_type=F32, **kw)


def split_three(u):
    a = u.astype(BF16).astype(F32)
    rest = u - a
    b = rest.astype(BF16).astype(F32)
    c = rest - b
    return a, b, c


def is_block(value, i):
    top, below = 1, 1
    for j in range(4):
        if j != i:
            top = top * (value - j)
            below = below * (i - j)
    return lax.div(top * (1 if below > 0 else -1), abs(below))


def factor_panel(ch, w, p):
    k = pl.multiple_of(p * 8, 8)
    shift = lax.rem(128 - k, 128)
    sub = lax.broadcasted_iota(jnp.int32, (8, 128), 0)
    for m in range(2):
        pa = ch[m, pl.ds(k, 8), 0:128]
        pw = ch[m, pl.ds(k, 8), 128:256]
        d = pltpu.roll(pa, shift, 1)
        c = [jnp.broadcast_to(d[:, j : j + 1], (8, 128)) for j in range(8)]
        scale = jnp.zeros((8, 128), F32)
        for j in range(8):
            pivot = jnp.broadcast_to(c[j][j : j + 1, :], (8, 128))
            root = lax.rsqrt(pivot)
            scale = jnp.where(sub == j, root, scale)
            if j < 7:
                f = jnp.where(sub > j, c[j] * (root * root), 0.0)
                pa = pa - f * jnp.broadcast_to(pa[j : j + 1, :], (8, 128))
                pw = pw - f * jnp.broadcast_to(pw[j : j + 1, :], (8, 128))
                for q in range(j + 1, 8):
                    c[q] = c[q] - f * jnp.broadcast_to(c[q][j : j + 1, :], (8, 128))
        ua = pa * scale
        uw = pw * scale
        w[m, pl.ds(k, 8), :] = uw
        a1, a2, a3 = split_three(ua)
        w1, w2, w3 = split_three(uw)
        left = jnp.concatenate([a1, a1, a2, a2, a1, a3], axis=0).astype(BF16)
        right = jnp.concatenate(
            [
                jnp.concatenate([a1, a2, a1, a2, a3, a1], axis=0),
                jnp.concatenate([w1, w2, w1, w2, w3, w1], axis=0),
            ],
            axis=1,
        ).astype(BF16)
        ch[m] = ch[m] - dot_tn(left, right)


def kernel(
    mass_hbm,
    mask_ref,
    modes_hbm,
    fixed_hbm,
    map_ref,
    gmass_hbm,
    tmass_hbm,
    gbasis_hbm,
    tbasis_hbm,
    coup_ref,
    gmodes_ref,
    tmodes_ref,
    gout_ref,
    apex_ref,
    raw,
    masked,
    cin,
    cp,
    loaded,
    fixed,
    maskrow,
    gmass,
    tmass,
    xall,
    part,
    gram,
    g_in,
    g_sum,
    g_all,
    t_in,
    t_sum,
    t_row,
    t_fin,
    t_all,
    opp1,
    own1,
    acc1,
    s1,
    opp2,
    own2,
    acc2,
    tcol,
    tcol_in,
    ch,
    winv,
    lsem,
    bsem,
    msem,
    x_send,
    x_recv,
    g1_send,
    g1_recv,
    g2_send,
    g2_recv,
    ta_send,
    ta_recv,
    tb_send,
    tb_recv,
    tc_send,
    tc_recv,
    r_send,
    r_recv,
    k_send,
    k_recv,
):
    r = lax.axis_index("row")
    c = lax.axis_index("col")
    z = lax.div(r, 4)
    x = lax.rem(r, 4)

    locals_ = [
        None,
        pltpu.make_async_copy(fixed_hbm, fixed, lsem.at[1]),
        pltpu.make_async_copy(gmass_hbm, gmass, lsem.at[2]),
        pltpu.make_async_copy(tmass_hbm, tmass, lsem.at[3]),
        pltpu.make_async_copy(gbasis_hbm, xall.at[r, 0], lsem.at[4]),
        pltpu.make_async_copy(tbasis_hbm, xall.at[r, 1], lsem.at[5]),
    ]
    blocks = [
        pltpu.make_async_copy(
            modes_hbm.at[:, pl.ds(b * TILE, TILE)], cin.at[b], bsem.at[b]
        )
        for b in range(8)
    ]
    chunks = [
        pltpu.make_async_copy(
            mass_hbm.at[pl.ds(i * CHUNK, CHUNK)], raw.at[pl.ds(i * CHUNK, CHUNK)], msem.at[i]
        )
        for i in range(CHUNKS)
    ]
    locals_[4].start()
    locals_[5].start()
    for b in range(8):
        blocks[b].start()
    chunks[0].start()
    chunks[1].start()
    locals_[2].start()
    locals_[3].start()
    for i in range(2, CHUNKS):
        chunks[i].start()
    locals_[1].start()

    barrier = pltpu.get_barrier_semaphore()

    @pl.loop(1, ROWS)
    def _(d):
        pl.semaphore_signal(
            barrier, inc=1, device_id=(lax.rem(r + d, ROWS), c), device_id_type=MESH
        )

    @pl.loop(1, COLS)
    def _(d):
        pl.semaphore_signal(
            barrier, inc=1, device_id=(r, lax.rem(c + d, COLS)), device_id_type=MESH
        )

    for b in range(16):
        maskrow[:, b * TILE : (b + 1) * TILE] = jnp.broadcast_to(
            mask_ref[:, b : b + 1].astype(F32), (16, TILE)
        )

    def apply_mask(i):
        chunks[i].wait()
        for half in range(2):
            rows = i * CHUNK + half * TILE
            a = i * 2 + half
            m = jnp.broadcast_to(maskrow[a : a + 1, :], (16, N)).astype(BF16)
            for q in range(TILE // 16):
                masked[i % 2, half * TILE + q * 16 : half * TILE + (q + 1) * 16, :] = (
                    raw[rows + q * 16 : rows + (q + 1) * 16, :] * m
                )

    for b in range(8):
        blocks[b].wait()
    for k in range(2):
        for i in range(4):
            at = 0
            for a in range(1, 4):
                at = at + a * is_block(map_ref[k, a], i)
            to = k * SEP + i * TILE
            cp[:, to : to + TILE] = cin[k * 4 + lax.rem(at, 4)]
    apply_mask(0)

    pl.semaphore_wait(barrier, ROWS - 1 + COLS - 1)
    locals_[4].wait()
    locals_[5].wait()

    def row_copy(d, src, dst, send, recv):
        return pltpu.make_async_remote_copy(
            src_ref=src,
            dst_ref=dst,
            send_sem=send.at[d],
            recv_sem=recv.at[d],
            device_id=(lax.rem(r + d, ROWS), c),
            device_id_type=MESH,
        )

    def col_copy(d, src, dst, send, recv):
        return pltpu.make_async_remote_copy(
            src_ref=src,
            dst_ref=dst,
            send_sem=send.at[d],
            recv_sem=recv.at[d],
            device_id=(r, lax.rem(c + d, COLS)),
            device_id_type=MESH,
        )

    def each_row(fn):
        @pl.loop(1, ROWS)
        def _(d):
            fn(d)

    def each_col(fn):
        @pl.loop(1, COLS)
        def _(d):
            fn(d)

    def src_row(d):
        return lax.rem(r + ROWS - d, ROWS)

    def src_col(d):
        return lax.rem(c + COLS - d, COLS)

    x_copy = lambda d: row_copy(d, xall.at[r], xall.at[r], x_send, x_recv)
    x_wait = lambda d: row_copy(d, xall.at[r], xall.at[src_row(d)], x_send, x_recv)
    each_row(lambda d: x_copy(d).start())

    for i in range(CHUNKS):
        if i + 1 < CHUNKS:
            apply_mask(i + 1)
        loaded[i * CHUNK : (i + 1) * CHUNK, :] = dot_nn(masked[i % 2], cp[...]).astype(BF16)

    each_row(lambda d: x_wait(d).wait_recv())

    part[0] = dot_tn(cp[:, 0:SEP], loaded[:, 0:SEP]).reshape(4, 4, 32, SEP)
    part[1] = dot_tn(cp[:, SEP:], loaded[:, SEP:]).reshape(4, 4, 32, SEP)
    locals_[2].wait()
    locals_[3].wait()
    part[0, z, x] = part[0, z, x] + gmass[...]
    own_rows = lax.div(lax.broadcasted_iota(jnp.int32, (32, SEP), 0), 4) == c
    own_top = jnp.concatenate([tmass[...]] * 8, axis=0)
    part[1, z, x] = part[1, z, x] + jnp.where(own_rows, own_top, 0.0)

    def basis(m):
        return xall[:, m].reshape(SEP, 128)

    for m in (1, 0):
        applied = dot_nn(part[m].reshape(SEP, SEP), basis(m), precision=HIGHEST)
        gram[m] = dot_tn(basis(m), applied, precision=HIGHEST)
        if m == 1:
            for q in range(COLS):
                t_row[q] = gram[1, q * 16 : (q + 1) * 16, :]
            each_col(
                lambda d: col_copy(
                    d, t_row.at[lax.rem(c + d, COLS)], t_in.at[c], ta_send, ta_recv
                ).start()
            )
    for q in range(ROWS):
        g_sum[q] = gram[0, q * 8 : (q + 1) * 8, :]
    each_row(
        lambda d: row_copy(
            d, g_sum.at[lax.rem(r + d, ROWS)], g_in.at[r], g1_send, g1_recv
        ).start()
    )
    t_in[c] = t_row[c]
    g_in[r] = g_sum[r]

    locals_[1].wait()
    projected = dot_tn(fixed[...], loaded[...])
    seen = [
        dot_nn(projected[:, m * SEP : (m + 1) * SEP], basis(m), precision=HIGHEST)
        for m in range(2)
    ]
    coup_ref[:, 0:128] = seen[0]
    coup_ref[:, 128:256] = seen[1]

    each_col(
        lambda d: col_copy(d, t_row.at[0], t_in.at[src_col(d)], ta_send, ta_recv).wait_recv()
    )
    total = t_in[0]
    for q in range(1, COLS):
        total = total + t_in[q]
    t_sum[r] = total
    each_row(lambda d: row_copy(d, t_sum.at[r], t_sum.at[r], tb_send, tb_recv).start())

    each_row(
        lambda d: row_copy(d, g_sum.at[0], g_in.at[src_row(d)], g1_send, g1_recv).wait_recv()
    )
    total = g_in[0]
    for q in range(1, ROWS):
        total = total + g_in[q]
    g_all[r] = total
    each_row(lambda d: row_copy(d, g_all.at[r], g_all.at[r], g2_send, g2_recv).start())

    def ring(phase, arr):
        along_z = (arr == 0) == (phase == 1)
        me = z if along_z else x

        def device(step):
            to = lax.rem(me + step + 4, 4)
            return (to * 4 + x, c) if along_z else (z * 4 + to, c)

        return me, device

    def source(phase, arr, dest, half):
        if phase == 1:
            if arr == 0:
                return part.at[0, dest, pl.ds(half * 2, 2)]
            return part.at[1, pl.ds(half * 2, 2), dest]
        return s1.at[arr, dest, pl.ds(half * 16, 16)]

    boxes = {1: (opp1, own1, acc1), 2: (opp2, own2, acc2)}

    def ring_copy(phase, arr, kind, way, src):
        _, device = ring(phase, arr)
        slot = ((phase - 1) * 2 + arr) * 6 + kind * 2 + way
        return pltpu.make_async_remote_copy(
            src_ref=src,
            dst_ref=boxes[phase][kind].at[arr, way],
            send_sem=r_send.at[slot],
            recv_sem=r_recv.at[slot],
            device_id=device(1 - 2 * way),
            device_id_type=MESH,
        )

    def opp_copy(phase, arr, way):
        me, _ = ring(phase, arr)
        return ring_copy(phase, arr, 0, way, source(phase, arr, lax.rem(me + 2, 4), way))

    def own_copy(phase, arr, way):
        me, _ = ring(phase, arr)
        dest = lax.rem(me + 1 - 2 * way + 4, 4)
        return ring_copy(phase, arr, 1, way, source(phase, arr, dest, 1 - way))

    def acc_copy(phase, arr, way):
        return ring_copy(phase, arr, 2, way, boxes[phase][0].at[arr, way])

    def ring_open(phase):
        for copy in (opp_copy, own_copy):
            for arr in range(2):
                for way in range(2):
                    copy(phase, arr, way).start()

    def ring_pass(phase):
        for arr in range(2):
            me, _ = ring(phase, arr)
            for way in range(2):
                opp_copy(phase, arr, way).wait_recv()
                dest = lax.rem(me + 1 - 2 * way + 4, 4)
                box = boxes[phase][0].at[arr, way]
                box[...] = box[...] + source(phase, arr, dest, way)[...]
                acc_copy(phase, arr, way).start()

    def ring_close(phase, arr):
        me, _ = ring(phase, arr)
        halves = []
        for half in range(2):
            acc_copy(phase, arr, half).wait_recv()
            own_copy(phase, arr, 1 - half).wait_recv()
            halves.append(
                source(phase, arr, me, half)[...]
                + boxes[phase][2][arr, half]
                + boxes[phase][1][arr, 1 - half]
            )
        return halves

    ring_open(1)

    each_row(
        lambda d: row_copy(d, t_sum.at[r], t_sum.at[src_row(d)], tb_send, tb_recv).wait_recv()
    )
    total = t_sum[0]
    for q in range(1, ROWS):
        total = total + t_sum[q]
    t_all[c] = total
    each_col(lambda d: col_copy(d, t_all.at[c], t_all.at[c], tc_send, tc_recv).start())

    each_row(
        lambda d: row_copy(d, g_all.at[r], g_all.at[src_row(d)], g2_send, g2_recv).wait_recv()
    )
    each_col(
        lambda d: col_copy(d, t_all.at[c], t_all.at[src_col(d)], tc_send, tc_recv).wait_recv()
    )
    eye = (
        lax.broadcasted_iota(jnp.int32, (128, 128), 0)
        == lax.broadcasted_iota(jnp.int32, (128, 128), 1)
    ).astype(F32)
    for m, whole in enumerate((g_all[...], t_all[...])):
        whole = whole.reshape(128, 128)
        ch[m, :, 0:128] = 0.5 * (whole + whole.T)
        ch[m, :, 128:256] = eye

    def panels(lo, hi):
        @pl.loop(lo, hi)
        def _(p):
            factor_panel(ch, winv, p)

    panels(0, 3)
    ring_pass(1)
    panels(3, 7)
    for arr in range(2):
        halves = ring_close(1, arr)
        s1[arr, 0:2] = halves[0]
        s1[arr, 2:4] = halves[1]
    ring_open(2)
    panels(7, 10)
    ring_pass(2)
    panels(10, 13)
    halves = ring_close(2, 1)
    for half in range(2):
        for q in range(4):
            tcol[half * 4 + q] = halves[half][q * 4 : (q + 1) * 4, :]
    each_col(
        lambda d: col_copy(
            d, tcol.at[lax.rem(c + d, COLS)], tcol_in.at[c], k_send, k_recv
        ).start()
    )
    tcol_in[c] = tcol[c]
    halves = ring_close(2, 0)
    for half in range(2):
        gout_ref[half * 16 : (half + 1) * 16, :] = SEP * halves[half]
    panels(13, 16)

    first = dot_nt(coup_ref[:, 0:128], winv[0], precision=HIGHEST)
    second = dot_nt(coup_ref[:, 128:256], winv[1], precision=HIGHEST)
    coup_ref[:, 0:128] = first
    coup_ref[:, 128:256] = second
    gmodes_ref[...] = dot_nt(xall[r, 0], winv[0], precision=HIGHEST)
    tmodes_ref[...] = dot_nt(xall[r, 1], winv[1], precision=HIGHEST)

    each_col(
        lambda d: col_copy(d, tcol.at[0], tcol_in.at[src_col(d)], k_send, k_recv).wait_recv()
    )
    total = tcol_in[0]
    for q in range(1, COLS):
        total = total + tcol_in[q]
    apex_ref[...] = SEP * total

    def sends_row(d):
        x_copy(d).wait_send()
        row_copy(d, g_sum.at[0], g_in.at[r], g1_send, g1_recv).wait_send()
        row_copy(d, g_all.at[r], g_all.at[r], g2_send, g2_recv).wait_send()
        row_copy(d, t_sum.at[r], t_sum.at[r], tb_send, tb_recv).wait_send()

    def sends_col(d):
        col_copy(d, t_row.at[0], t_in.at[c], ta_send, ta_recv).wait_send()
        col_copy(d, t_all.at[c], t_all.at[c], tc_send, tc_recv).wait_send()
        col_copy(d, tcol.at[0], tcol_in.at[c], k_send, k_recv).wait_send()

    each_row(sends_row)
    each_col(sends_col)
    for phase in (1, 2):
        for copy in (opp_copy, own_copy, acc_copy):
            for arr in range(2):
                for way in range(2):
                    copy(phase, arr, way).wait_send()


def body(
    leaf_mass,
    tile_mask,
    constraint_modes,
    leaf_fixed_modes,
    block_map,
    group_mass,
    top_mass,
    group_basis,
    top_basis,
):
    hbm = pl.BlockSpec(memory_space=pl.ANY)
    vmem = pl.BlockSpec(memory_space=pltpu.VMEM)
    smem = pl.BlockSpec(memory_space=pltpu.SMEM)
    dma = pltpu.SemaphoreType.DMA
    half1 = (2, 2, 2, 32, SEP)
    half2 = (2, 2, 16, SEP)
    scratch = [
        pltpu.VMEM((N, N), BF16),
        pltpu.VMEM((2, CHUNK, N), BF16),
        pltpu.VMEM((8, N, TILE), BF16),
        pltpu.VMEM((N, 2 * SEP), BF16),
        pltpu.VMEM((N, 2 * SEP), BF16),
        pltpu.VMEM((N, 128), BF16),
        pltpu.VMEM((16, N), F32),
        pltpu.VMEM((32, SEP), F32),
        pltpu.VMEM((4, SEP), F32),
        pltpu.VMEM((ROWS, 2, 32, 128), F32),
        pltpu.VMEM((2, 4, 4, 32, SEP), F32),
        pltpu.VMEM((2, 128, 128), F32),
        pltpu.VMEM((ROWS, 8, 128), F32),
        pltpu.VMEM((ROWS, 8, 128), F32),
        pltpu.VMEM((ROWS, 8, 128), F32),
        pltpu.VMEM((COLS, 16, 128), F32),
        pltpu.VMEM((ROWS, 16, 128), F32),
        pltpu.VMEM((COLS, 16, 128), F32),
        pltpu.VMEM((COLS, 16, 128), F32),
        pltpu.VMEM((COLS, 16, 128), F32),
        pltpu.VMEM(half1, F32),
        pltpu.VMEM(half1, F32),
        pltpu.VMEM(half1, F32),
        pltpu.VMEM((2, 4, 32, SEP), F32),
        pltpu.VMEM(half2, F32),
        pltpu.VMEM(half2, F32),
        pltpu.VMEM(half2, F32),
        pltpu.VMEM((COLS, 4, SEP), F32),
        pltpu.VMEM((COLS, 4, SEP), F32),
        pltpu.VMEM((2, 128, 256), F32),
        pltpu.VMEM((2, 128, 128), F32),
        dma((6,)),
        dma((8,)),
        dma((CHUNKS,)),
        dma((ROWS,)),
        dma((ROWS,)),
        dma((ROWS,)),
        dma((ROWS,)),
        dma((ROWS,)),
        dma((ROWS,)),
        dma((COLS,)),
        dma((COLS,)),
        dma((ROWS,)),
        dma((ROWS,)),
        dma((COLS,)),
        dma((COLS,)),
        dma((24,)),
        dma((24,)),
        dma((COLS,)),
        dma((COLS,)),
    ]
    coupling, gmodes, tmodes, gout, apex = pl.pallas_call(
        kernel,
        out_shape=(
            jax.ShapeDtypeStruct((128, 256), F32),
            jax.ShapeDtypeStruct((32, 128), F32),
            jax.ShapeDtypeStruct((32, 128), F32),
            jax.ShapeDtypeStruct((32, SEP), F32),
            jax.ShapeDtypeStruct((4, SEP), F32),
        ),
        in_specs=[hbm, vmem, hbm, hbm, smem, hbm, hbm, hbm, hbm],
        out_specs=(vmem, vmem, vmem, vmem, vmem),
        scratch_shapes=scratch,
        compiler_params=pltpu.CompilerParams(
            collective_id=0, has_side_effects=True, vmem_limit_bytes=60 << 20
        ),
        name="assemble",
    )(
        leaf_mass[0],
        tile_mask[0],
        constraint_modes[0],
        leaf_fixed_modes[0],
        block_map[0],
        group_mass[0],
        top_mass,
        group_basis[0],
        top_basis,
    )
    return (coupling.reshape(1, 128, 2, 128), gmodes[None], tmodes, gout[None], apex)


def solution(mesh):
    in_specs = (
        P(("row", "col"), None, None),
        P(("row", "col"), None, None),
        P(("row", "col"), None, None),
        P(("row", "col"), None, None),
        P(("row", "col"), None, None),
        P("col", "row", None),
        P(("row", "col"), None),
        P("col", "row", None),
        P("row", None),
    )
    out_specs = (
        P(("row", "col"), None, None, None),
        P("col", "row", None),
        P("row", None),
        P("col", "row", None),
        P(("row", "col"), None),
    )
    return jax.shard_map(body, mesh=mesh, in_specs=in_specs, out_specs=out_specs, check_vma=False)
```

time: 216 us -> 70.3 us (0.33)
  waiting for transfers between devices: 75 us -> 0 us
  Pallas kernels: 0 us -> 62.2 us
  other arithmetic: 53.8 us -> 0 us
  local copies, waits for them, and re-layouts: 34.9 us -> 7.04 us
  matrix products: 26.8 us -> 0 us
  starting transfers between devices: 22.9 us -> 0 us
    all_to_all x4 -> x0, waiting for transfers between devices: 75 us -> none  [the longest x3 44 us: copy_for_each(): lax.all_to_all(jnp.broadcast_to(value[None], (peers, *value.shape)), axis...]
    pallas_call x0 -> x1, Pallas kernels: none -> 62.2 us  [body(): pl.pallas_call(kernel, out_shape=(jax.ShapeDtypeStruct((128, 256), F32),...]
    another operation x10 -> x0, other arithmetic: 45.9 us -> none  [the longest x6 25 us: from_gram(): lower_factor = jnp.linalg.cholesky(gram_matrix)]
    dot_general x10 -> x0, matrix products: 26 us -> none  [the longest x1 15.9 us: body(): jnp.dot(masked, modes_c, preferred_element_type=jnp.float32)]
    all_to_all x4 -> x0, starting transfers between devices: 22.9 us -> none  [the longest x3 14.3 us: copy_for_each(): lax.all_to_all(jnp.broadcast_to(value[None], (peers, *value.shape)), axis...]
    mul x4 -> x0, local copies, waits for them, and re-layouts: 17.9 us -> none  [the longest x2 17.7 us: body(): leaf_matrix.reshape(tile_count, TILE, tile_count, TILE)]
    gather x8 -> x0, local copies, waits for them, and re-layouts: 4.95 us -> none  [the longest x6 3.82 us: to_separator(): blocks = blocks[inverse][:, :, inverse]]
    broadcast_in_dim x3 -> x0, local copies, waits for them, and re-layouts: 4.64 us -> none  [copy_for_each(): jnp.broadcast_to(value[None], (peers, *value.shape))]
  transfers between devices with their start and end apart: 4 -> 0, of which waited for: 4 -> 0; matrix products, arithmetic and copies ran while one was open for 3% -> 0% of each run, Pallas kernels for 0% -> 0%
where the time goes in v1:
time: 70.3 us; the launch traced here: 69.9 us
  Pallas kernels  62.2 us (88%)
  local copies, waits for them, and re-layouts  7.04 us (10%)
    pallas_call x1, Pallas kernels, body(): pl.pallas_call(kernel, out_shape=(jax.ShapeDtypeStruct((128, 256), F32),...  62.2 us
    unnamed x4, local copies, waits for them, and re-layouts  5.41 us
    reshape x1, local copies, waits for them, and re-layouts, body(): coupling.reshape(1, 128, 2, 128)  1.62 us

profile of v1, /device:TPU:1, one launch (start us, length us, event | category | flops | bytes accessed | tf_op | source)
XLA Modules:
  0.0 69.9 jit_solution(4262228992213475291)
XLA Ops:
  0.6 62.2 %assemble.1 = (f32[128,256]{1,0:T(8,128)}, f32[32,128]{1,0:T(8,128)}, f32[32,128]{1,0:T(8,128)}, f32[32,512]{1,0:T(8,128)}, f32[4,512]{1,0:T(4,128)}) custom-call(bf16[2048,2048]{1,0:T(8,128)(2,1)} %bitcast.9, s32[16,16]{1,0:T(8,128)} %bitcast.16, bf16[2048,1024]{1,0:T(8,128)(2,1)} %bitcast.10, bf16[2048,128]{1,0:T(8,128)(2,1)} %bitcast.11, ...), custom_call_target="tpu_custom_call" | custom-call | tf_op jit(solution)/shard_map/assemble/pallas_call | solution.py:574
  62.9 1.6 %reshape.13 = f32[1,128,2,128]{3,2,1,0:T(2,128)} reshape(f32[128,256]{1,0:T(8,128)} %get-tuple-element.10) | data formatting | bytes 262144 | tf_op jit(solution)/shard_map/reshape | solution.py:601
  64.5 1.3 %copy.18 = f32[1,32,128]{2,1,0:T(8,128)} copy(f32[1,32,128]{2,1,0:T(8,128)} %bitcast.15) | data formatting | bytes 32768
  65.8 1.3 %copy.19 = f32[32,128]{1,0:T(8,128)} copy(f32[32,128]{1,0:T(8,128)} %get-tuple-element.22) | data formatting | bytes 32768
  67.1 1.5 %copy.20 = f32[1,32,512]{2,1,0:T(8,128)} copy(f32[1,32,512]{2,1,0:T(8,128)} %bitcast.13) | data formatting | bytes 131072
  68.6 1.3 %copy.21 = f32[4,512]{1,0:T(4,128)} copy(f32[4,512]{1,0:T(4,128)} %get-tuple-element.24) | data formatting | bytes 16384

commit v2 on v1

--- a/solution.py
+++ b/solution.py
@@ -10,7 +10,7 @@
 ROWS = 16
 COLS = 8
 N = 2048
-CHUNK = 256
+CHUNK = 1024
 CHUNKS = N // CHUNK
 F32 = jnp.float32
 BF16 = jnp.bfloat16
@@ -48,14 +48,12 @@
 
 
 def factor_panel(ch, w, p):
-    k = pl.multiple_of(p * 8, 8)
-    shift = lax.rem(128 - k, 128)
+    k = p * 8
     sub = lax.broadcasted_iota(jnp.int32, (8, 128), 0)
     for m in range(2):
-        pa = ch[m, pl.ds(k, 8), 0:128]
-        pw = ch[m, pl.ds(k, 8), 128:256]
-        d = pltpu.roll(pa, shift, 1)
-        c = [jnp.broadcast_to(d[:, j : j + 1], (8, 128)) for j in range(8)]
+        pa = ch[m, k : k + 8, 0:128]
+        pw = ch[m, k : k + 8, 128:256]
+        c = [jnp.broadcast_to(pa[:, k + j : k + j + 1], (8, 128)) for j in range(8)]
         scale = jnp.zeros((8, 128), F32)
         for j in range(8):
             pivot = jnp.broadcast_to(c[j][j : j + 1, :], (8, 128))
@@ -69,7 +67,9 @@
                     c[q] = c[q] - f * jnp.broadcast_to(c[q][j : j + 1, :], (8, 128))
         ua = pa * scale
         uw = pw * scale
-        w[m, pl.ds(k, 8), :] = uw
+        w[m, k : k + 8, :] = uw
+        if p == 15:
+            continue
         a1, a2, a3 = split_three(ua)
         w1, w2, w3 = split_three(uw)
         left = jnp.concatenate([a1, a1, a2, a2, a1, a3], axis=0).astype(BF16)
@@ -80,7 +80,12 @@
             ],
             axis=1,
         ).astype(BF16)
-        ch[m] = ch[m] - dot_tn(left, right)
+        ch[m, k + 8 :] = ch[m, k + 8 :] - dot_tn(left, right)[k + 8 :]
+
+
+def split_two(v):
+    high = v.astype(BF16)
+    return high, (v - high.astype(F32)).astype(BF16)
 
 
 def kernel(
@@ -93,9 +98,9 @@
     tmass_hbm,
     gbasis_hbm,
     tbasis_hbm,
-    coup_ref,
-    gmodes_ref,
-    tmodes_ref,
+    seen_ref,
+    w_ref,
+    own_ref,
     gout_ref,
     apex_ref,
     raw,
@@ -128,7 +133,6 @@
     tcol,
     tcol_in,
     ch,
-    winv,
     lsem,
     bsem,
     msem,
@@ -207,9 +211,9 @@
 
     def apply_mask(i):
         chunks[i].wait()
-        for half in range(2):
+        for half in range(CHUNK // TILE):
             rows = i * CHUNK + half * TILE
-            a = i * 2 + half
+            a = i * (CHUNK // TILE) + half
             m = jnp.broadcast_to(maskrow[a : a + 1, :], (16, N)).astype(BF16)
             for q in range(TILE // 16):
                 masked[i % 2, half * TILE + q * 16 : half * TILE + (q + 1) * 16, :] = (
@@ -287,12 +291,90 @@
     own_top = jnp.concatenate([tmass[...]] * 8, axis=0)
     part[1, z, x] = part[1, z, x] + jnp.where(own_rows, own_top, 0.0)
 
+    def ring(phase, arr):
+        along_z = (arr == 0) == (phase == 1)
+        me = z if along_z else x
+
+        def device(step):
+            to = lax.rem(me + step + 4, 4)
+            return (to * 4 + x, c) if along_z else (z * 4 + to, c)
+
+        return me, device
+
+    def source(phase, arr, dest, half):
+        if phase == 1:
+            if arr == 0:
+                return part.at[0, dest, pl.ds(half * 2, 2)]
+            return part.at[1, pl.ds(half * 2, 2), dest]
+        return s1.at[arr, dest, pl.ds(half * 16, 16)]
+
+    boxes = {1: (opp1, own1, acc1), 2: (opp2, own2, acc2)}
+
+    def ring_copy(phase, arr, kind, way, src):
+        _, device = ring(phase, arr)
+        slot = ((phase - 1) * 2 + arr) * 6 + kind * 2 + way
+        return pltpu.make_async_remote_copy(
+            src_ref=src,
+            dst_ref=boxes[phase][kind].at[arr, way],
+            send_sem=r_send.at[slot],
+            recv_sem=r_recv.at[slot],
+            device_id=device(1 - 2 * way),
+            device_id_type=MESH,
+        )
+
+    def opp_copy(phase, arr, way):
+        me, _ = ring(phase, arr)
+        return ring_copy(phase, arr, 0, way, source(phase, arr, lax.rem(me + 2, 4), way))
+
+    def own_copy(phase, arr, way):
+        me, _ = ring(phase, arr)
+        dest = lax.rem(me + 1 - 2 * way + 4, 4)
+        return ring_copy(phase, arr, 1, way, source(phase, arr, dest, 1 - way))
+
+    def acc_copy(phase, arr, way):
+        return ring_copy(phase, arr, 2, way, boxes[phase][0].at[arr, way])
+
+    def ring_open(phase, copies):
+        for copy in copies:
+            for arr in range(2):
+                for way in range(2):
+                    copy(phase, arr, way).start()
+
+    def ring_pass(phase):
+        for arr in range(2):
+            me, _ = ring(phase, arr)
+            for way in range(2):
+                opp_copy(phase, arr, way).wait_recv()
+                dest = lax.rem(me + 1 - 2 * way + 4, 4)
+                box = boxes[phase][0].at[arr, way]
+                box[...] = box[...] + source(phase, arr, dest, way)[...]
+                acc_copy(phase, arr, way).start()
+
+    def ring_close(phase, arr):
+        me, _ = ring(phase, arr)
+        halves = []
+        for half in range(2):
+            acc_copy(phase, arr, half).wait_recv()
+            own_copy(phase, arr, 1 - half).wait_recv()
+            halves.append(
+                source(phase, arr, me, half)[...]
+                + boxes[phase][2][arr, half]
+                + boxes[phase][1][arr, 1 - half]
+            )
+        return halves
+
     def basis(m):
         return xall[:, m].reshape(SEP, 128)
 
     for m in (1, 0):
-        applied = dot_nn(part[m].reshape(SEP, SEP), basis(m), precision=HIGHEST)
-        gram[m] = dot_tn(basis(m), applied, precision=HIGHEST)
+        x_high, x_low = split_two(basis(m))
+        x_both = jnp.concatenate([x_high, x_low], axis=1)
+        p_high, p_low = split_two(part[m].reshape(SEP, SEP))
+        applied = dot_nn(p_high, x_both)
+        applied = applied[:, 0:128] + applied[:, 128:256] + dot_nn(p_low, x_high)
+        a_high, a_low = split_two(applied)
+        term = dot_tn(x_both, a_high)
+        gram[m] = term[0:128] + term[128:256] + dot_tn(x_high, a_low)
         if m == 1:
             for q in range(COLS):
                 t_row[q] = gram[1, q * 16 : (q + 1) * 16, :]
@@ -311,14 +393,16 @@
     t_in[c] = t_row[c]
     g_in[r] = g_sum[r]
 
+    ring_open(1, (opp_copy,))
+
     locals_[1].wait()
     projected = dot_tn(fixed[...], loaded[...])
     seen = [
         dot_nn(projected[:, m * SEP : (m + 1) * SEP], basis(m), precision=HIGHEST)
         for m in range(2)
     ]
-    coup_ref[:, 0:128] = seen[0]
-    coup_ref[:, 128:256] = seen[1]
+    for m in range(2):
+        seen_ref[m] = seen[m]
 
     each_col(
         lambda d: col_copy(d, t_row.at[0], t_in.at[src_col(d)], ta_send, ta_recv).wait_recv()
@@ -338,79 +422,8 @@
     g_all[r] = total
     each_row(lambda d: row_copy(d, g_all.at[r], g_all.at[r], g2_send, g2_recv).start())
 
-    def ring(phase, arr):
-        along_z = (arr == 0) == (phase == 1)
-        me = z if along_z else x
-
-        def device(step):
-            to = lax.rem(me + step + 4, 4)
-            return (to * 4 + x, c) if along_z else (z * 4 + to, c)
-
-        return me, device
-
-    def source(phase, arr, dest, half):
-        if phase == 1:
-            if arr == 0:
-                return part.at[0, dest, pl.ds(half * 2, 2)]
-            return part.at[1, pl.ds(half * 2, 2), dest]
-        return s1.at[arr, dest, pl.ds(half * 16, 16)]
-
-    boxes = {1: (opp1, own1, acc1), 2: (opp2, own2, acc2)}
-
-    def ring_copy(phase, arr, kind, way, src):
-        _, device = ring(phase, arr)
-        slot = ((phase - 1) * 2 + arr) * 6 + kind * 2 + way
-        return pltpu.make_async_remote_copy(
-            src_ref=src,
-            dst_ref=boxes[phase][kind].at[arr, way],
-            send_sem=r_send.at[slot],
-            recv_sem=r_recv.at[slot],
-            device_id=device(1 - 2 * way),
-            device_id_type=MESH,
-        )
-
-    def opp_copy(phase, arr, way):
-        me, _ = ring(phase, arr)
-        return ring_copy(phase, arr, 0, way, source(phase, arr, lax.rem(me + 2, 4), way))
-
-    def own_copy(phase, arr, way):
-        me, _ = ring(phase, arr)
-        dest = lax.rem(me + 1 - 2 * way + 4, 4)
-        return ring_copy(phase, arr, 1, way, source(phase, arr, dest, 1 - way))
-
-    def acc_copy(phase, arr, way):
-        return ring_copy(phase, arr, 2, way, boxes[phase][0].at[arr, way])
-
-    def ring_open(phase):
-        for copy in (opp_copy, own_copy):
-            for arr in range(2):
-                for way in range(2):
-                    copy(phase, arr, way).start()
-
-    def ring_pass(phase):
-        for arr in range(2):
-            me, _ = ring(phase, arr)
-            for way in range(2):
-                opp_copy(phase, arr, way).wait_recv()
-                dest = lax.rem(me + 1 - 2 * way + 4, 4)
-                box = boxes[phase][0].at[arr, way]
-                box[...] = box[...] + source(phase, arr, dest, way)[...]
-                acc_copy(phase, arr, way).start()
-
-    def ring_close(phase, arr):
-        me, _ = ring(phase, arr)
-        halves = []
-        for half in range(2):
-            acc_copy(phase, arr, half).wait_recv()
-            own_copy(phase, arr, 1 - half).wait_recv()
-            halves.append(
-                source(phase, arr, me, half)[...]
-                + boxes[phase][2][arr, half]
-                + boxes[phase][1][arr, 1 - half]
-            )
-        return halves
-
-    ring_open(1)
+    ring_open(1, (own_copy,))
+    ring_pass(1)
 
     each_row(
         lambda d: row_copy(d, t_sum.at[r], t_sum.at[src_row(d)], tb_send, tb_recv).wait_recv()
@@ -437,21 +450,18 @@
         ch[m, :, 128:256] = eye
 
     def panels(lo, hi):
-        @pl.loop(lo, hi)
-        def _(p):
-            factor_panel(ch, winv, p)
-
-    panels(0, 3)
-    ring_pass(1)
-    panels(3, 7)
-    for arr in range(2):
+        for p in range(lo, hi):
+            factor_panel(ch, w_ref, p)
+
+    panels(0, 5)
+    for arr in (1, 0):
         halves = ring_close(1, arr)
         s1[arr, 0:2] = halves[0]
         s1[arr, 2:4] = halves[1]
-    ring_open(2)
-    panels(7, 10)
+    ring_open(2, (opp_copy, own_copy))
+    panels(5, 11)
     ring_pass(2)
-    panels(10, 13)
+    panels(11, 16)
     halves = ring_close(2, 1)
     for half in range(2):
         for q in range(4):
@@ -465,14 +475,7 @@
     halves = ring_close(2, 0)
     for half in range(2):
         gout_ref[half * 16 : (half + 1) * 16, :] = SEP * halves[half]
-    panels(13, 16)
-
-    first = dot_nt(coup_ref[:, 0:128], winv[0], precision=HIGHEST)
-    second = dot_nt(coup_ref[:, 128:256], winv[1], precision=HIGHEST)
-    coup_ref[:, 0:128] = first
-    coup_ref[:, 128:256] = second
-    gmodes_ref[...] = dot_nt(xall[r, 0], winv[0], precision=HIGHEST)
-    tmodes_ref[...] = dot_nt(xall[r, 1], winv[1], precision=HIGHEST)
+    own_ref[...] = xall[r]
 
     each_col(
         lambda d: col_copy(d, tcol.at[0], tcol_in.at[src_col(d)], k_send, k_recv).wait_recv()
@@ -500,6 +503,14 @@
             for arr in range(2):
                 for way in range(2):
                     copy(phase, arr, way).wait_send()
+
+
+def finish(seen, inverse, own, gmatrix, tmatrix, coup, gmodes, tmodes, gout, apex):
+    gout[...] = gmatrix[...]
+    apex[...] = tmatrix[...]
+    for m, modes in enumerate((gmodes, tmodes)):
+        coup[:, m, :] = dot_nt(seen[m], inverse[m], precision=HIGHEST)
+        modes[...] = dot_nt(own[m], inverse[m], precision=HIGHEST)
 
 
 def body(
@@ -550,7 +561,6 @@
         pltpu.VMEM((COLS, 4, SEP), F32),
         pltpu.VMEM((COLS, 4, SEP), F32),
         pltpu.VMEM((2, 128, 256), F32),
-        pltpu.VMEM((2, 128, 128), F32),
         dma((6,)),
         dma((8,)),
         dma((CHUNKS,)),
@@ -571,12 +581,12 @@
         dma((COLS,)),
         dma((COLS,)),
     ]
-    coupling, gmodes, tmodes, gout, apex = pl.pallas_call(
+    seen, inverse, own, gout, apex = pl.pallas_call(
         kernel,
         out_shape=(
-            jax.ShapeDtypeStruct((128, 256), F32),
-            jax.ShapeDtypeStruct((32, 128), F32),
-            jax.ShapeDtypeStruct((32, 128), F32),
+            jax.ShapeDtypeStruct((2, 128, 128), F32),
+            jax.ShapeDtypeStruct((2, 128, 128), F32),
+            jax.ShapeDtypeStruct((2, 32, 128), F32),
             jax.ShapeDtypeStruct((32, SEP), F32),
             jax.ShapeDtypeStruct((4, SEP), F32),
         ),
@@ -598,7 +608,20 @@
         group_basis[0],
         top_basis,
     )
-    return (coupling.reshape(1, 128, 2, 128), gmodes[None], tmodes, gout[None], apex)
+    coupling, gmodes, tmodes, gout, apex = pl.pallas_call(
+        finish,
+        out_shape=(
+            jax.ShapeDtypeStruct((128, 2, 128), F32),
+            jax.ShapeDtypeStruct((32, 128), F32),
+            jax.ShapeDtypeStruct((32, 128), F32),
+            jax.ShapeDtypeStruct((32, SEP), F32),
+            jax.ShapeDtypeStruct((4, SEP), F32),
+        ),
+        in_specs=[vmem] * 5,
+        out_specs=(vmem,) * 5,
+        name="finish",
+    )(seen, inverse, own, gout, apex)
+    return (coupling[None], gmodes[None], tmodes, gout[None], apex)
 
 
 def solution(mesh):

time: 70.3 us -> 55.2 us (0.79)
  Pallas kernels: 62.2 us -> 54.4 us
  local copies, waits for them, and re-layouts: 7.04 us -> 0 us
    pallas_call x1 -> x2, Pallas kernels: 62.2 us -> 54.4 us  [the longest x1 52.1 us: body(): pl.pallas_call(kernel, out_shape=(jax.ShapeDtypeStruct((2, 128, 128), F32...]
    unnamed x4 -> x0, local copies, waits for them, and re-layouts: 5.41 us -> none
    reshape x1 -> x0, local copies, waits for them, and re-layouts: 1.62 us -> none  [body(): coupling.reshape(1, 128, 2, 128)]
where the time goes in v2:
time: 55.2 us; the launch traced here: 55 us
  Pallas kernels  54.4 us (99%)
  between operations  0.64 us (1%)
    pallas_call x1, Pallas kernels, body(): pl.pallas_call(kernel, out_shape=(jax.ShapeDtypeStruct((2, 128, 128), F32...  52.1 us
    pallas_call x1, Pallas kernels, body(): pl.pallas_call(finish, out_shape=(jax.ShapeDtypeStruct((128, 2, 128), F32...  2.26 us

profile of v2, /device:TPU:1, one launch (start us, length us, event | category | flops | bytes accessed | tf_op | source)
XLA Modules:
  0.0 55.0 jit_solution(1209677563610142015)
XLA Ops:
  0.6 52.1 %assemble.1 = (f32[2,128,128]{2,1,0:T(8,128)}, f32[2,128,128]{2,1,0:T(8,128)}, f32[2,32,128]{2,1,0:T(8,128)}, f32[32,512]{1,0:T(8,128)}, f32[4,512]{1,0:T(4,128)}) custom-call(bf16[2048,2048]{1,0:T(8,128)(2,1)} %bitcast.10, s32[16,16]{1,0:T(8,128)} %bitcast.15, bf16[2048,1024]{1,0:T(8,128)(2,1)} %bitcast.11, bf16[2048,128]{1,0:T(8,128)(2,1)} %bitcast.12, ...), custom_call_target="tpu_custom_call" | custom-call | tf_op jit(solution)/shard_map/assemble/pallas_call | solution.py:584
  52.7 2.3 %finish.1 = (f32[128,2,128]{2,1,0:T(2,128)}, f32[32,128]{1,0:T(8,128)}, f32[32,128]{1,0:T(8,128)}, f32[32,512]{1,0:T(8,128)}, f32[4,512]{1,0:T(4,128)}) custom-call(f32[2,128,128]{2,1,0:T(8,128)} %get-tuple-element.15.seen, f32[2,128,128]{2,1,0:T(8,128)} %get-tuple-element.16.inverse, f32[2,32,128]{2,1,0:T(8,128)} %get-tuple-element.17.own, ...), custom_call_target="tpu_custom_call" | custom-call | tf_op jit(solution)/shard_map/finish/pallas_call | solution.py:611

commit v3 on v2

--- a/solution.py
+++ b/solution.py
@@ -9,6 +9,7 @@
 SEP = 512
 ROWS = 16
 COLS = 8
+PLANE = 32
 N = 2048
 CHUNK = 1024
 CHUNKS = N // CHUNK
@@ -113,7 +114,9 @@
     gmass,
     tmass,
     xall,
-    part,
+    pg,
+    pt,
+    swapped,
     gram,
     g_in,
     g_sum,
@@ -123,13 +126,16 @@
     t_row,
     t_fin,
     t_all,
-    opp1,
-    own1,
-    acc1,
-    s1,
-    opp2,
-    own2,
-    acc2,
+    opp1g,
+    own1g,
+    acc1g,
+    opp1t,
+    own1t,
+    acc1t,
+    sg,
+    opp2g,
+    own2g,
+    acc2g,
     tcol,
     tcol_in,
     ch,
@@ -152,11 +158,14 @@
     r_recv,
     k_send,
     k_recv,
+    w_sem,
 ):
     r = lax.axis_index("row")
     c = lax.axis_index("col")
     z = lax.div(r, 4)
     x = lax.rem(r, 4)
+    slot = z * COLS + c
+    core = lax.rem(c, 2)
 
     locals_ = [
         None,
@@ -198,11 +207,16 @@
             barrier, inc=1, device_id=(lax.rem(r + d, ROWS), c), device_id_type=MESH
         )
 
-    @pl.loop(1, COLS)
-    def _(d):
-        pl.semaphore_signal(
-            barrier, inc=1, device_id=(r, lax.rem(c + d, COLS)), device_id_type=MESH
-        )
+    @pl.loop(0, 4)
+    def _(up):
+        @pl.loop(1, COLS)
+        def _(d):
+            pl.semaphore_signal(
+                barrier,
+                inc=1,
+                device_id=(lax.rem(z + up, 4) * 4 + x, lax.rem(c + d, COLS)),
+                device_id_type=MESH,
+            )
 
     for b in range(16):
         maskrow[:, b * TILE : (b + 1) * TILE] = jnp.broadcast_to(
@@ -216,7 +230,7 @@
             a = i * (CHUNK // TILE) + half
             m = jnp.broadcast_to(maskrow[a : a + 1, :], (16, N)).astype(BF16)
             for q in range(TILE // 16):
-                masked[i % 2, half * TILE + q * 16 : half * TILE + (q + 1) * 16, :] = (
+                masked[i, half * TILE + q * 16 : half * TILE + (q + 1) * 16, :] = (
                     raw[rows + q * 16 : rows + (q + 1) * 16, :] * m
                 )
 
@@ -231,10 +245,6 @@
             cp[:, to : to + TILE] = cin[k * 4 + lax.rem(at, 4)]
     apply_mask(0)
 
-    pl.semaphore_wait(barrier, ROWS - 1 + COLS - 1)
-    locals_[4].wait()
-    locals_[5].wait()
-
     def row_copy(d, src, dst, send, recv):
         return pltpu.make_async_remote_copy(
             src_ref=src,
@@ -271,25 +281,42 @@
     def src_col(d):
         return lax.rem(c + COLS - d, COLS)
 
-    x_copy = lambda d: row_copy(d, xall.at[r], xall.at[r], x_send, x_recv)
-    x_wait = lambda d: row_copy(d, xall.at[r], xall.at[src_row(d)], x_send, x_recv)
-    each_row(lambda d: x_copy(d).start())
-
-    for i in range(CHUNKS):
-        if i + 1 < CHUNKS:
-            apply_mask(i + 1)
-        loaded[i * CHUNK : (i + 1) * CHUNK, :] = dot_nn(masked[i % 2], cp[...]).astype(BF16)
-
-    each_row(lambda d: x_wait(d).wait_recv())
-
-    part[0] = dot_tn(cp[:, 0:SEP], loaded[:, 0:SEP]).reshape(4, 4, 32, SEP)
-    part[1] = dot_tn(cp[:, SEP:], loaded[:, SEP:]).reshape(4, 4, 32, SEP)
-    locals_[2].wait()
-    locals_[3].wait()
-    part[0, z, x] = part[0, z, x] + gmass[...]
-    own_rows = lax.div(lax.broadcasted_iota(jnp.int32, (32, SEP), 0), 4) == c
-    own_top = jnp.concatenate([tmass[...]] * 8, axis=0)
-    part[1, z, x] = part[1, z, x] + jnp.where(own_rows, own_top, 0.0)
+    def x_copy(d, m, at):
+        return pltpu.make_async_remote_copy(
+            src_ref=xall.at[r, m],
+            dst_ref=xall.at[at, m],
+            send_sem=x_send.at[m, d],
+            recv_sem=x_recv.at[m, d],
+            device_id=(lax.rem(r + d, ROWS), c),
+            device_id_type=MESH,
+        )
+
+    def k_copy(d, at):
+        s = lax.rem(slot + d, PLANE)
+        return pltpu.make_async_remote_copy(
+            src_ref=tcol.at[s],
+            dst_ref=tcol_in.at[at],
+            send_sem=k_send.at[d],
+            recv_sem=k_recv.at[d],
+            device_id=(lax.div(s, COLS) * 4 + x, lax.rem(s, COLS)),
+            device_id_type=MESH,
+        )
+    def load_columns(i, m):
+        cols = slice(m * SEP, (m + 1) * SEP)
+        loaded[i * CHUNK : (i + 1) * CHUNK, cols] = dot_nn(masked[i], cp[:, cols]).astype(BF16)
+
+    def basis(m):
+        return xall[:, m].reshape(SEP, 128)
+
+    def gram_of(matrix, m):
+        x_high, x_low = split_two(basis(m))
+        x_both = jnp.concatenate([x_high, x_low], axis=1)
+        p_high, p_low = split_two(matrix)
+        applied = dot_nn(p_high, x_both)
+        applied = applied[:, 0:128] + applied[:, 128:256] + dot_nn(p_low, x_high)
+        a_high, a_low = split_two(applied)
+        term = dot_tn(x_both, a_high)
+        gram[m] = term[0:128] + term[128:256] + dot_tn(x_high, a_low)
 
     def ring(phase, arr):
         along_z = (arr == 0) == (phase == 1)
@@ -304,20 +331,31 @@
     def source(phase, arr, dest, half):
         if phase == 1:
             if arr == 0:
-                return part.at[0, dest, pl.ds(half * 2, 2)]
-            return part.at[1, pl.ds(half * 2, 2), dest]
-        return s1.at[arr, dest, pl.ds(half * 16, 16)]
-
-    boxes = {1: (opp1, own1, acc1), 2: (opp2, own2, acc2)}
+                return pg.at[0, dest, pl.ds(half * 2, 2)]
+            if arr == 2:
+                return pg.at[1, pl.ds(half * 2, 2), dest]
+            return pt.at[core, pl.ds(half * 2, 2), dest]
+        return sg.at[arr // 2, dest, pl.ds(half * 16, 16)]
+
+    boxes = {
+        (1, 0): (opp1g, own1g, acc1g),
+        (1, 1): (opp1t, own1t, acc1t),
+        (2, 0): (opp2g, own2g, acc2g),
+    }
+
+    def box_of(phase, arr, kind, way):
+        if arr == 1:
+            return boxes[phase, 1][kind].at[way]
+        return boxes[phase, 0][kind].at[arr // 2, way]
 
     def ring_copy(phase, arr, kind, way, src):
         _, device = ring(phase, arr)
-        slot = ((phase - 1) * 2 + arr) * 6 + kind * 2 + way
+        sem = ((phase - 1) * 3 + arr) * 6 + kind * 2 + way
         return pltpu.make_async_remote_copy(
             src_ref=src,
-            dst_ref=boxes[phase][kind].at[arr, way],
-            send_sem=r_send.at[slot],
-            recv_sem=r_recv.at[slot],
+            dst_ref=box_of(phase, arr, kind, way),
+            send_sem=r_send.at[sem],
+            recv_sem=r_recv.at[sem],
             device_id=device(1 - 2 * way),
             device_id_type=MESH,
         )
@@ -332,21 +370,20 @@
         return ring_copy(phase, arr, 1, way, source(phase, arr, dest, 1 - way))
 
     def acc_copy(phase, arr, way):
-        return ring_copy(phase, arr, 2, way, boxes[phase][0].at[arr, way])
-
-    def ring_open(phase, copies):
-        for copy in copies:
-            for arr in range(2):
-                for way in range(2):
-                    copy(phase, arr, way).start()
-
-    def ring_pass(phase):
-        for arr in range(2):
+        return ring_copy(phase, arr, 2, way, box_of(phase, arr, 0, way))
+
+    def ring_start(phase, arrs, copy):
+        for arr in arrs:
+            for way in range(2):
+                copy(phase, arr, way).start()
+
+    def ring_pass(phase, arrs):
+        for arr in arrs:
             me, _ = ring(phase, arr)
             for way in range(2):
                 opp_copy(phase, arr, way).wait_recv()
                 dest = lax.rem(me + 1 - 2 * way + 4, 4)
-                box = boxes[phase][0].at[arr, way]
+                box = box_of(phase, arr, 0, way)
                 box[...] = box[...] + source(phase, arr, dest, way)[...]
                 acc_copy(phase, arr, way).start()
 
@@ -358,31 +395,64 @@
             own_copy(phase, arr, 1 - half).wait_recv()
             halves.append(
                 source(phase, arr, me, half)[...]
-                + boxes[phase][2][arr, half]
-                + boxes[phase][1][arr, 1 - half]
+                + box_of(phase, arr, 2, half)[...]
+                + box_of(phase, arr, 1, 1 - half)[...]
             )
         return halves
 
-    def basis(m):
-        return xall[:, m].reshape(SEP, 128)
-
-    for m in (1, 0):
-        x_high, x_low = split_two(basis(m))
-        x_both = jnp.concatenate([x_high, x_low], axis=1)
-        p_high, p_low = split_two(part[m].reshape(SEP, SEP))
-        applied = dot_nn(p_high, x_both)
-        applied = applied[:, 0:128] + applied[:, 128:256] + dot_nn(p_low, x_high)
-        a_high, a_low = split_two(applied)
-        term = dot_tn(x_both, a_high)
-        gram[m] = term[0:128] + term[128:256] + dot_tn(x_high, a_low)
-        if m == 1:
-            for q in range(COLS):
-                t_row[q] = gram[1, q * 16 : (q + 1) * 16, :]
-            each_col(
-                lambda d: col_copy(
-                    d, t_row.at[lax.rem(c + d, COLS)], t_in.at[c], ta_send, ta_recv
-                ).start()
-            )
+    load_columns(0, 1)
+    pl.semaphore_wait(barrier, ROWS - 1 + 4 * (COLS - 1))
+    locals_[5].wait()
+    each_row(lambda d: x_copy(d, 1, r).start())
+    locals_[4].wait()
+    each_row(lambda d: x_copy(d, 0, r).start())
+    apply_mask(1)
+    load_columns(1, 1)
+    load_columns(0, 0)
+    load_columns(1, 0)
+    top = dot_tn(cp[:, SEP:], loaded[:, SEP:])
+    for h in range(2):
+        pt[h] = top[:, h * 256 : (h + 1) * 256].reshape(4, 4, 32, 256)
+    locals_[3].wait()
+    own_rows = lax.div(lax.broadcasted_iota(jnp.int32, (32, 256), 0), 4) == c
+    own_top = jnp.concatenate([tmass[...]] * 8, axis=0)
+    for h in range(2):
+        pt[h, z, x] = pt[h, z, x] + jnp.where(own_rows, own_top[:, h * 256 : (h + 1) * 256], 0.0)
+    swap = pltpu.make_async_remote_copy(
+        src_ref=pt.at[1 - core],
+        dst_ref=swapped,
+        send_sem=w_sem.at[0],
+        recv_sem=w_sem.at[1],
+        device_id=(r, c + 1 - 2 * core),
+        device_id_type=MESH,
+    )
+    swap.start()
+    each_row(lambda d: x_copy(d, 1, src_row(d)).wait_recv())
+    gram_of(
+        jnp.concatenate([pt[0].reshape(SEP, 256), pt[1].reshape(SEP, 256)], axis=1), 1
+    )
+    for q in range(COLS):
+        t_row[q] = gram[1, q * 16 : (q + 1) * 16, :]
+    each_col(
+        lambda d: col_copy(
+            d, t_row.at[lax.rem(c + d, COLS)], t_in.at[c], ta_send, ta_recv
+        ).start()
+    )
+    t_in[c] = t_row[c]
+    swap.wait_recv()
+    pt[core] = pt[core] + swapped[...]
+    ring_start(1, (1,), opp_copy)
+
+    group = dot_tn(cp[:, 0:SEP], loaded[:, 0:SEP])
+    for h in range(2):
+        pg[h] = group[:, h * 256 : (h + 1) * 256].reshape(4, 4, 32, 256)
+    locals_[2].wait()
+    for h in range(2):
+        pg[h, z, x] = pg[h, z, x] + gmass[:, h * 256 : (h + 1) * 256]
+    each_row(lambda d: x_copy(d, 0, src_row(d)).wait_recv())
+    gram_of(
+        jnp.concatenate([pg[0].reshape(SEP, 256), pg[1].reshape(SEP, 256)], axis=1), 0
+    )
     for q in range(ROWS):
         g_sum[q] = gram[0, q * 8 : (q + 1) * 8, :]
     each_row(
@@ -390,19 +460,16 @@
             d, g_sum.at[lax.rem(r + d, ROWS)], g_in.at[r], g1_send, g1_recv
         ).start()
     )
-    t_in[c] = t_row[c]
     g_in[r] = g_sum[r]
-
-    ring_open(1, (opp_copy,))
+    ring_start(1, (0, 2), opp_copy)
 
     locals_[1].wait()
     projected = dot_tn(fixed[...], loaded[...])
-    seen = [
-        dot_nn(projected[:, m * SEP : (m + 1) * SEP], basis(m), precision=HIGHEST)
-        for m in range(2)
-    ]
     for m in range(2):
-        seen_ref[m] = seen[m]
+        seen_ref[m] = dot_nn(
+            projected[:, m * SEP : (m + 1) * SEP], basis(m), precision=HIGHEST
+        )
+    own_ref[...] = xall[r]
 
     each_col(
         lambda d: col_copy(d, t_row.at[0], t_in.at[src_col(d)], ta_send, ta_recv).wait_recv()
@@ -412,6 +479,7 @@
         total = total + t_in[q]
     t_sum[r] = total
     each_row(lambda d: row_copy(d, t_sum.at[r], t_sum.at[r], tb_send, tb_recv).start())
+    ring_start(1, (1,), own_copy)
 
     each_row(
         lambda d: row_copy(d, g_sum.at[0], g_in.at[src_row(d)], g1_send, g1_recv).wait_recv()
@@ -421,9 +489,8 @@
         total = total + g_in[q]
     g_all[r] = total
     each_row(lambda d: row_copy(d, g_all.at[r], g_all.at[r], g2_send, g2_recv).start())
-
-    ring_open(1, (own_copy,))
-    ring_pass(1)
+    ring_start(1, (0, 2), own_copy)
+    ring_pass(1, (1, 0, 2))
 
     each_row(
         lambda d: row_copy(d, t_sum.at[r], t_sum.at[src_row(d)], tb_send, tb_recv).wait_recv()
@@ -434,17 +501,12 @@
     t_all[c] = total
     each_col(lambda d: col_copy(d, t_all.at[c], t_all.at[c], tc_send, tc_recv).start())
 
-    each_row(
-        lambda d: row_copy(d, g_all.at[r], g_all.at[src_row(d)], g2_send, g2_recv).wait_recv()
-    )
-    each_col(
-        lambda d: col_copy(d, t_all.at[c], t_all.at[src_col(d)], tc_send, tc_recv).wait_recv()
-    )
     eye = (
         lax.broadcasted_iota(jnp.int32, (128, 128), 0)
         == lax.broadcasted_iota(jnp.int32, (128, 128), 1)
     ).astype(F32)
-    for m, whole in enumerate((g_all[...], t_all[...])):
+
+    def start_factor(m, whole):
         whole = whole.reshape(128, 128)
         ch[m, :, 0:128] = 0.5 * (whole + whole.T)
         ch[m, :, 128:256] = eye
@@ -453,40 +515,54 @@
         for p in range(lo, hi):
             factor_panel(ch, w_ref, p)
 
-    panels(0, 5)
-    for arr in (1, 0):
+    for arr in (0, 2):
         halves = ring_close(1, arr)
-        s1[arr, 0:2] = halves[0]
-        s1[arr, 2:4] = halves[1]
-    ring_open(2, (opp_copy, own_copy))
-    panels(5, 11)
-    ring_pass(2)
-    panels(11, 16)
-    halves = ring_close(2, 1)
+        sg[arr // 2, 0:2] = halves[0]
+        sg[arr // 2, 2:4] = halves[1]
+    ring_start(2, (0, 2), opp_copy)
+    ring_start(2, (0, 2), own_copy)
+
+    each_row(
+        lambda d: row_copy(d, g_all.at[r], g_all.at[src_row(d)], g2_send, g2_recv).wait_recv()
+    )
+    start_factor(0, g_all[...])
+    each_col(
+        lambda d: col_copy(d, t_all.at[c], t_all.at[src_col(d)], tc_send, tc_recv).wait_recv()
+    )
+    start_factor(1, t_all[...])
+
+    halves = ring_close(1, 1)
     for half in range(2):
-        for q in range(4):
-            tcol[half * 4 + q] = halves[half][q * 4 : (q + 1) * 4, :]
-    each_col(
-        lambda d: col_copy(
-            d, tcol.at[lax.rem(c + d, COLS)], tcol_in.at[c], k_send, k_recv
-        ).start()
-    )
-    tcol_in[c] = tcol[c]
-    halves = ring_close(2, 0)
-    for half in range(2):
-        gout_ref[half * 16 : (half + 1) * 16, :] = SEP * halves[half]
-    own_ref[...] = xall[r]
-
-    each_col(
-        lambda d: col_copy(d, tcol.at[0], tcol_in.at[src_col(d)], k_send, k_recv).wait_recv()
-    )
-    total = tcol_in[0]
-    for q in range(1, COLS):
-        total = total + tcol_in[q]
-    apex_ref[...] = SEP * total
+        for i in range(2):
+            for q in range(COLS):
+                tcol[(half * 2 + i) * COLS + q] = halves[half][i, q * 4 : (q + 1) * 4, :]
+
+    @pl.loop(1, PLANE)
+    def _(d):
+        k_copy(d, slot).start()
+
+    tcol_in[slot] = tcol[slot]
+    panels(0, 8)
+    ring_pass(2, (0, 2))
+    panels(8, 16)
+    for arr in (0, 2):
+        halves = ring_close(2, arr)
+        for half in range(2):
+            gout_ref[half * 16 : (half + 1) * 16, arr * 128 : arr * 128 + 256] = SEP * halves[half]
+
+    @pl.loop(1, PLANE)
+    def _(d):
+        k_copy(d, lax.rem(slot + PLANE - d, PLANE)).wait_recv()
+
+    for h in range(2):
+        total = tcol_in[h]
+        for q in range(h + 2, PLANE, 2):
+            total = total + tcol_in[q]
+        apex_ref[:, h * 256 : (h + 1) * 256] = SEP * total
 
     def sends_row(d):
-        x_copy(d).wait_send()
+        x_copy(d, 0, r).wait_send()
+        x_copy(d, 1, r).wait_send()
         row_copy(d, g_sum.at[0], g_in.at[r], g1_send, g1_recv).wait_send()
         row_copy(d, g_all.at[r], g_all.at[r], g2_send, g2_recv).wait_send()
         row_copy(d, t_sum.at[r], t_sum.at[r], tb_send, tb_recv).wait_send()
@@ -494,13 +570,18 @@
     def sends_col(d):
         col_copy(d, t_row.at[0], t_in.at[c], ta_send, ta_recv).wait_send()
         col_copy(d, t_all.at[c], t_all.at[c], tc_send, tc_recv).wait_send()
-        col_copy(d, tcol.at[0], tcol_in.at[c], k_send, k_recv).wait_send()
-
+
+    swap.wait_send()
     each_row(sends_row)
     each_col(sends_col)
-    for phase in (1, 2):
+
+    @pl.loop(1, PLANE)
+    def _(d):
+        k_copy(d, slot).wait_send()
+
+    for phase, arrs in ((1, (0, 1, 2)), (2, (0, 2))):
         for copy in (opp_copy, own_copy, acc_copy):
-            for arr in range(2):
+            for arr in arrs:
                 for way in range(2):
                     copy(phase, arr, way).wait_send()
 
@@ -528,8 +609,9 @@
     vmem = pl.BlockSpec(memory_space=pltpu.VMEM)
     smem = pl.BlockSpec(memory_space=pltpu.SMEM)
     dma = pltpu.SemaphoreType.DMA
-    half1 = (2, 2, 2, 32, SEP)
-    half2 = (2, 2, 16, SEP)
+    half1g = (2, 2, 2, 32, SEP // 2)
+    half1t = (2, 2, 32, SEP // 2)
+    half2g = (2, 2, 16, SEP // 2)
     scratch = [
         pltpu.VMEM((N, N), BF16),
         pltpu.VMEM((2, CHUNK, N), BF16),
@@ -541,7 +623,9 @@
         pltpu.VMEM((32, SEP), F32),
         pltpu.VMEM((4, SEP), F32),
         pltpu.VMEM((ROWS, 2, 32, 128), F32),
-        pltpu.VMEM((2, 4, 4, 32, SEP), F32),
+        pltpu.VMEM((2, 4, 4, 32, SEP // 2), F32),
+        pltpu.VMEM((2, 4, 4, 32, SEP // 2), F32),
+        pltpu.VMEM((4, 4, 32, SEP // 2), F32),
         pltpu.VMEM((2, 128, 128), F32),
         pltpu.VMEM((ROWS, 8, 128), F32),
         pltpu.VMEM((ROWS, 8, 128), F32),
@@ -551,21 +635,24 @@
         pltpu.VMEM((COLS, 16, 128), F32),
         pltpu.VMEM((COLS, 16, 128), F32),
         pltpu.VMEM((COLS, 16, 128), F32),
-        pltpu.VMEM(half1, F32),
-        pltpu.VMEM(half1, F32),
-        pltpu.VMEM(half1, F32),
-        pltpu.VMEM((2, 4, 32, SEP), F32),
-        pltpu.VMEM(half2, F32),
-        pltpu.VMEM(half2, F32),
-        pltpu.VMEM(half2, F32),
-        pltpu.VMEM((COLS, 4, SEP), F32),
-        pltpu.VMEM((COLS, 4, SEP), F32),
+        pltpu.VMEM(half1g, F32),
+        pltpu.VMEM(half1g, F32),
+        pltpu.VMEM(half1g, F32),
+        pltpu.VMEM(half1t, F32),
+        pltpu.VMEM(half1t, F32),
+        pltpu.VMEM(half1t, F32),
+        pltpu.VMEM((2, 4, 32, SEP // 2), F32),
+        pltpu.VMEM(half2g, F32),
+        pltpu.VMEM(half2g, F32),
+        pltpu.VMEM(half2g, F32),
+        pltpu.VMEM((PLANE, 4, SEP // 2), F32),
+        pltpu.VMEM((PLANE, 4, SEP // 2), F32),
         pltpu.VMEM((2, 128, 256), F32),
         dma((6,)),
         dma((8,)),
         dma((CHUNKS,)),
-        dma((ROWS,)),
-        dma((ROWS,)),
+        dma((2, ROWS)),
+        dma((2, ROWS)),
         dma((ROWS,)),
         dma((ROWS,)),
         dma((ROWS,)),
@@ -576,10 +663,11 @@
         dma((ROWS,)),
         dma((COLS,)),
         dma((COLS,)),
-        dma((24,)),
-        dma((24,)),
-        dma((COLS,)),
-        dma((COLS,)),
+        dma((36,)),
+        dma((36,)),
+        dma((PLANE,)),
+        dma((PLANE,)),
+        dma((2,)),
     ]
     seen, inverse, own, gout, apex = pl.pallas_call(
         kernel,

time: 55.2 us -> 51.6 us (0.935)
  Pallas kernels: 54.4 us -> 50.8 us
    pallas_call x1, Pallas kernels: 52.1 us -> 48.5 us  [body(): pl.pallas_call(kernel, out_shape=(jax.ShapeDtypeStruct((2, 128, 128), F32...]
where the time goes in v3:
time: 51.6 us; the launch traced here: 51.4 us
  Pallas kernels  50.8 us (98%)
  between operations  0.64 us (1%)
    pallas_call x1, Pallas kernels, body(): pl.pallas_call(kernel, out_shape=(jax.ShapeDtypeStruct((2, 128, 128), F32...  48.5 us
    pallas_call x1, Pallas kernels, body(): pl.pallas_call(finish, out_shape=(jax.ShapeDtypeStruct((128, 2, 128), F32...  2.26 us

profile of v3, /device:TPU:1, one launch (start us, length us, event | category | flops | bytes accessed | tf_op | source)
XLA Modules:
  0.0 51.4 jit_solution(4841223096569198454)
XLA Ops:
  0.6 48.5 %assemble.1 = (f32[2,128,128]{2,1,0:T(8,128)}, f32[2,128,128]{2,1,0:T(8,128)}, f32[2,32,128]{2,1,0:T(8,128)}, f32[32,512]{1,0:T(8,128)}, f32[4,512]{1,0:T(4,128)}) custom-call(bf16[2048,2048]{1,0:T(8,128)(2,1)} %bitcast.10, s32[16,16]{1,0:T(8,128)} %bitcast.15, bf16[2048,1024]{1,0:T(8,128)(2,1)} %bitcast.11, bf16[2048,128]{1,0:T(8,128)(2,1)} %bitcast.12, ...), custom_call_target="tpu_custom_call" | custom-call | tf_op jit(solution)/shard_map/assemble/pallas_call | solution.py:672
  49.1 2.3 %finish.1 = (f32[128,2,128]{2,1,0:T(2,128)}, f32[32,128]{1,0:T(8,128)}, f32[32,128]{1,0:T(8,128)}, f32[32,512]{1,0:T(8,128)}, f32[4,512]{1,0:T(4,128)}) custom-call(f32[2,128,128]{2,1,0:T(8,128)} %get-tuple-element.15.seen, f32[2,128,128]{2,1,0:T(8,128)} %get-tuple-element.16.inverse, f32[2,32,128]{2,1,0:T(8,128)} %get-tuple-element.17.own, ...), custom_call_target="tpu_custom_call" | custom-call | tf_op jit(solution)/shard_map/finish/pallas_call | solution.py:699

commit v4 on v3

--- a/solution.py
+++ b/solution.py
@@ -480,6 +480,7 @@
     t_sum[r] = total
     each_row(lambda d: row_copy(d, t_sum.at[r], t_sum.at[r], tb_send, tb_recv).start())
     ring_start(1, (1,), own_copy)
+    ring_pass(1, (1,))
 
     each_row(
         lambda d: row_copy(d, g_sum.at[0], g_in.at[src_row(d)], g1_send, g1_recv).wait_recv()
@@ -490,7 +491,7 @@
     g_all[r] = total
     each_row(lambda d: row_copy(d, g_all.at[r], g_all.at[r], g2_send, g2_recv).start())
     ring_start(1, (0, 2), own_copy)
-    ring_pass(1, (1, 0, 2))
+    ring_pass(1, (0, 2))
 
     each_row(
         lambda d: row_copy(d, t_sum.at[r], t_sum.at[src_row(d)], tb_send, tb_recv).wait_recv()
@@ -515,6 +516,17 @@
         for p in range(lo, hi):
             factor_panel(ch, w_ref, p)
 
+    halves = ring_close(1, 1)
+    for half in range(2):
+        for i in range(2):
+            for q in range(COLS):
+                tcol[(half * 2 + i) * COLS + q] = halves[half][i, q * 4 : (q + 1) * 4, :]
+
+    @pl.loop(1, PLANE)
+    def _(d):
+        k_copy(d, slot).start()
+
+    tcol_in[slot] = tcol[slot]
     for arr in (0, 2):
         halves = ring_close(1, arr)
         sg[arr // 2, 0:2] = halves[0]
@@ -531,17 +543,6 @@
     )
     start_factor(1, t_all[...])
 
-    halves = ring_close(1, 1)
-    for half in range(2):
-        for i in range(2):
-            for q in range(COLS):
-                tcol[(half * 2 + i) * COLS + q] = halves[half][i, q * 4 : (q + 1) * 4, :]
-
-    @pl.loop(1, PLANE)
-    def _(d):
-        k_copy(d, slot).start()
-
-    tcol_in[slot] = tcol[slot]
     panels(0, 8)
     ring_pass(2, (0, 2))
     panels(8, 16)

time: 51.6 us -> 50.8 us (0.984)
  Pallas kernels: 50.8 us -> 49.8 us
    pallas_call x1, Pallas kernels: 48.5 us -> 47.5 us  [body(): pl.pallas_call(kernel, out_shape=(jax.ShapeDtypeStruct((2, 128, 128), F32...]
where the time goes in v4:
time: 50.8 us; the launch traced here: 50.4 us
  Pallas kernels  49.8 us (98%)
  between operations  0.64 us (1%)
    pallas_call x1, Pallas kernels, body(): pl.pallas_call(kernel, out_shape=(jax.ShapeDtypeStruct((2, 128, 128), F32...  47.5 us
    pallas_call x1, Pallas kernels, body(): pl.pallas_call(finish, out_shape=(jax.ShapeDtypeStruct((128, 2, 128), F32...  2.26 us

profile of v4, /device:TPU:1, one launch (start us, length us, event | category | flops | bytes accessed | tf_op | source)
XLA Modules:
  0.0 50.4 jit_solution(10900270124424330024)
XLA Ops:
  0.6 47.5 %assemble.1 = (f32[2,128,128]{2,1,0:T(8,128)}, f32[2,128,128]{2,1,0:T(8,128)}, f32[2,32,128]{2,1,0:T(8,128)}, f32[32,512]{1,0:T(8,128)}, f32[4,512]{1,0:T(4,128)}) custom-call(bf16[2048,2048]{1,0:T(8,128)(2,1)} %bitcast.10, s32[16,16]{1,0:T(8,128)} %bitcast.15, bf16[2048,1024]{1,0:T(8,128)(2,1)} %bitcast.11, bf16[2048,128]{1,0:T(8,128)(2,1)} %bitcast.12, ...), custom_call_target="tpu_custom_call" | custom-call | tf_op jit(solution)/shard_map/assemble/pallas_call | solution.py:673
  48.2 2.3 %finish.1 = (f32[128,2,128]{2,1,0:T(2,128)}, f32[32,128]{1,0:T(8,128)}, f32[32,128]{1,0:T(8,128)}, f32[32,512]{1,0:T(8,128)}, f32[4,512]{1,0:T(4,128)}) custom-call(f32[2,128,128]{2,1,0:T(8,128)} %get-tuple-element.15.seen, f32[2,128,128]{2,1,0:T(8,128)} %get-tuple-element.16.inverse, f32[2,32,128]{2,1,0:T(8,128)} %get-tuple-element.17.own, ...), custom_call_target="tpu_custom_call" | custom-call | tf_op jit(solution)/shard_map/finish/pallas_call | solution.py:700
